TPU v7x, 128 devices: a whole 4x4x4 slice. The times are simulated.
128 devices in a mesh: dp: 8 (over z_lo, x), seq: 16 (over z_hi, y, core).
Axes of the slice: x: 4, y: 4, z: 4 (z_hi: 2, z_lo: 2; z = z_hi * 2 + z_lo), core: 2. Of those that a mesh axis runs over, the one named last changes fastest.
Arguments:
- series: bfloat16 [8, 8192, 128], P('dp', 'seq'), may hold values from -6 to 6
- cotangent: bfloat16 [8, 8192, 128], P('dp', 'seq'), may hold values from -6 to 6
- w_in: bfloat16 [128, 384], replicated, may hold values from -0.5 to 0.5
- w_out: bfloat16 [128, 128], replicated, may hold values from -0.5 to 0.5
- taps: float32 [3, 384], replicated, may hold values from -3 to 3
- skip_one: float32 [128], replicated, may hold values from 0.5 to 1.5
- skip_two: float32 [128], replicated, may hold values from 0.5 to 1.5
- filter_one: float32 [8, 8192], P(None, 'seq'), may hold values from -0.0625 to 0.0625
- filter_two: float32 [8, 8192], P(None, 'seq'), may hold values from -0.0625 to 0.0625
Outputs:
- output: bfloat16 [8, 8192, 128], P('dp', 'seq')
- d_series: bfloat16 [8, 8192, 128], P('dp', 'seq')
- grad_w_in: float32 [128, 384], replicated
- grad_w_out: float32 [128, 128], replicated
- grad_taps: float32 [3, 384], replicated
- grad_skip_one: float32 [128], replicated
- grad_skip_two: float32 [128], replicated
- grad_filter_one: float32 [8, 8192], P(None, 'seq')
- grad_filter_two: float32 [8, 8192], P(None, 'seq')
All inputs are finite; a program needn't handle non-finite values.
Results may differ from a plain program's by a relative error of at most 0.015.
Values may be sent and summed in bfloat16 or wider, within the bound.
A program may use at most 128 MiB of HBM per device.

v0:
```python
import math
import jax
import jax.numpy as jnp
from jax import lax
from jax.sharding import PartitionSpec as P

FACTOR = 32


def passed_along(block, axis, distance):
    devices = range(lax.axis_size(axis))
    route = [(i - distance, i) for i in devices if i - distance in devices]
    return lax.ppermute(block, axis, route)


def grid_index(shape_pair, along):
    return lax.broadcasted_iota(jnp.int32, shape_pair, along)


def twiddle(row_index, col_index, period, direction):
    angle = (
        direction * 2.0 * math.pi / period * (row_index * col_index % period).astype(jnp.float32)
    )
    return (jnp.cos(angle), jnp.sin(angle))


def complex_mul(left_real, left_imag, right_real, right_imag):
    return (
        left_real * right_real - left_imag * right_imag,
        left_real * right_imag + left_imag * right_real,
    )


def complex_dft(real_part, imag_part, table_real, table_imag, pattern):
    highest = lax.Precision.HIGHEST
    first = jnp.einsum(pattern, table_real, real_part, precision=highest)
    second = jnp.einsum(pattern, table_imag, imag_part, precision=highest)
    third = jnp.einsum(pattern, table_real, imag_part, precision=highest)
    fourth = jnp.einsum(pattern, table_imag, real_part, precision=highest)
    return (first - second, third + fourth)


def local_dft(pieces):
    real_part, imag_part = pieces
    series_count, pair_rows, block_rows, channels = real_part.shape
    inner = block_rows // FACTOR
    real_part = real_part.reshape(series_count, pair_rows, FACTOR, inner, channels)
    imag_part = imag_part.reshape(series_count, pair_rows, FACTOR, inner, channels)
    table_real, table_imag = twiddle(
        grid_index((FACTOR, FACTOR), 0), grid_index((FACTOR, FACTOR), 1), FACTOR, -1.0
    )
    real_part, imag_part = complex_dft(
        real_part, imag_part, table_real, table_imag, "ca,erabk->ercbk"
    )
    turn_real, turn_imag = twiddle(
        grid_index((FACTOR, inner), 0), grid_index((FACTOR, inner), 1), block_rows, -1.0
    )
    real_part, imag_part = complex_mul(
        real_part, imag_part, turn_real[:, :, None], turn_imag[:, :, None]
    )
    table_real, table_imag = twiddle(
        grid_index((inner, inner), 0), grid_index((inner, inner), 1), inner, -1.0
    )
    return complex_dft(real_part, imag_part, table_real, table_imag, "db,ercbk->ercdk")


def local_inverse(real_part, imag_part):
    series_count, pair_rows, outer, inner, channels = real_part.shape
    block_rows = outer * inner
    table_real, table_imag = twiddle(
        grid_index((inner, inner), 0), grid_index((inner, inner), 1), inner, 1.0
    )
    real_part, imag_part = complex_dft(
        real_part, imag_part, table_real, table_imag, "bd,ercdk->ercbk"
    )
    turn_real, turn_imag = twiddle(
        grid_index((outer, inner), 0), grid_index((outer, inner), 1), block_rows, 1.0
    )
    real_part, imag_part = complex_mul(
        real_part, imag_part, turn_real[:, :, None], turn_imag[:, :, None]
    )
    table_real, table_imag = twiddle(
        grid_index((outer, outer), 0), grid_index((outer, outer), 1), outer, 1.0
    )
    real_part, imag_part = complex_dft(
        real_part, imag_part, table_real, table_imag, "ac,ercbk->erabk"
    )
    return (
        real_part.reshape(series_count, pair_rows, block_rows, channels),
        imag_part.reshape(series_count, pair_rows, block_rows, channels),
    )


def first_section(columns):
    highest = lax.Precision.HIGHEST
    groups = lax.axis_size("seq")
    column_width = columns.shape[2]
    period = 2 * groups * groups * column_width
    offset = lax.axis_index("seq") * column_width
    table_real, table_imag = twiddle(
        grid_index((2 * groups, groups), 0), grid_index((2 * groups, groups), 1), 2 * groups, -1.0
    )
    real_part = jnp.einsum("kn,enjc->ekjc", table_real, columns, precision=highest)
    imag_part = jnp.einsum("kn,enjc->ekjc", table_imag, columns, precision=highest)
    turn_real, turn_imag = twiddle(
        grid_index((2 * groups, column_width), 0),
        grid_index((2 * groups, column_width), 1) + offset,
        period,
        -1.0,
    )
    return complex_mul(real_part, imag_part, turn_real[:, :, None], turn_imag[:, :, None])


def last_section(pieces):
    highest = lax.Precision.HIGHEST
    part_real, part_imag = pieces
    groups = lax.axis_size("seq")
    column_width = part_real.shape[2]
    period = 2 * groups * groups * column_width
    offset = lax.axis_index("seq") * column_width
    turn_real, turn_imag = twiddle(
        grid_index((2 * groups, column_width), 0),
        grid_index((2 * groups, column_width), 1) + offset,
        period,
        1.0,
    )
    part_real, part_imag = complex_mul(
        part_real, part_imag, turn_real[:, :, None], turn_imag[:, :, None]
    )
    table_real, table_imag = twiddle(
        grid_index((groups, 2 * groups), 0), grid_index((groups, 2 * groups), 1), 2 * groups, 1.0
    )
    summed = jnp.einsum("nk,ekjc->enjc", table_real, part_real, precision=highest) - jnp.einsum(
        "nk,ekjc->enjc", table_imag, part_imag, precision=highest
    )
    return summed * (1.0 / period)


def to_frequency(real_part, imag_part):
    return local_dft(
        (
            lax.all_to_all(real_part, "seq", split_axis=1, concat_axis=2, tiled=True),
            lax.all_to_all(imag_part, "seq", split_axis=1, concat_axis=2, tiled=True),
        )
    )


def spectrum(field):
    real_part, imag_part = first_section(
        lax.all_to_all(field, "seq", split_axis=2, concat_axis=1, tiled=True)
    )
    return to_frequency(real_part, imag_part)


def signal(real_part, imag_part):
    real_part, imag_part = local_inverse(real_part, imag_part)
    columns = last_section(
        (
            lax.all_to_all(real_part, "seq", split_axis=2, concat_axis=1, tiled=True),
            lax.all_to_all(imag_part, "seq", split_axis=2, concat_axis=1, tiled=True),
        )
    )
    return lax.all_to_all(columns, "seq", split_axis=1, concat_axis=2, tiled=True)


def order_spectrum(real_part, imag_part):
    series_count, pair_rows, outer, inner, channels = real_part.shape
    block_rows = outer * inner
    real_part = jnp.swapaxes(real_part, 2, 3).reshape(series_count, pair_rows, block_rows, channels)
    imag_part = jnp.swapaxes(imag_part, 2, 3).reshape(series_count, pair_rows, block_rows, channels)
    real_part, imag_part = (
        lax.all_to_all(real_part, "seq", split_axis=2, concat_axis=1, tiled=True),
        lax.all_to_all(imag_part, "seq", split_axis=2, concat_axis=1, tiled=True),
    )
    return (jnp.swapaxes(real_part, 1, 2), jnp.swapaxes(imag_part, 1, 2))


def restore_spectrum(real_part, imag_part):
    real_part = jnp.swapaxes(real_part, 1, 2)
    imag_part = jnp.swapaxes(imag_part, 1, 2)
    real_part, imag_part = (
        lax.all_to_all(real_part, "seq", split_axis=1, concat_axis=2, tiled=True),
        lax.all_to_all(imag_part, "seq", split_axis=1, concat_axis=2, tiled=True),
    )
    series_count, pair_rows, block_rows, channels = real_part.shape
    inner = block_rows // FACTOR
    real_part = jnp.swapaxes(
        real_part.reshape(series_count, pair_rows, inner, FACTOR, channels), 2, 3
    )
    imag_part = jnp.swapaxes(
        imag_part.reshape(series_count, pair_rows, inner, FACTOR, channels), 2, 3
    )
    return (real_part, imag_part)


def transform(field):
    real_part, imag_part = spectrum(field)
    real_part, imag_part = order_spectrum(real_part, imag_part)
    return (real_part, imag_part)


def untransform(real_part, imag_part, in_columns):
    real_part, imag_part = restore_spectrum(real_part, imag_part)
    return signal(real_part, imag_part)


def widen_groups(pieces, channels):
    real_part, imag_part = pieces
    repeat_count = channels // real_part.shape[-1]
    return (
        jnp.repeat(real_part, repeat_count, axis=-1),
        jnp.repeat(imag_part, repeat_count, axis=-1),
    )


def group_sum(pieces, filters):
    result = []
    for piece in pieces:
        channels = piece.shape[-1]
        reshaped = piece.reshape(piece.shape[:-1] + (filters, channels // filters))
        result.append(jnp.sum(jnp.sum(reshaped, axis=-1), axis=0, keepdims=True))
    return (result[0], result[1])


def rows_before(field):
    return passed_along(field[:, :, -2:], "seq", 1)


def rows_after(field):
    return passed_along(field[:, :, :2], "seq", -1)


def filter_blocks(filter_rows):
    return filter_rows.T.reshape(1, 1, filter_rows.shape[1], filter_rows.shape[0])


def shards(series, cotangent, w_in, w_out, taps, skip_one, skip_two, filter_one, filter_two):
    series_count, block_rows, width_d = series.shape
    filters = filter_one.shape[0]
    token_total = series_count * lax.axis_size("dp") * block_rows * lax.axis_size("seq")
    grad_scale = 1.0 / math.sqrt(token_total)
    series_four = series.reshape(series_count, 1, block_rows, width_d)
    cot_four = cotangent.reshape(series_count, 1, block_rows, width_d)
    series_here, cot_here = (series_four, cot_four)
    projected = jnp.einsum("entd,dc->entc", series_here, w_in, preferred_element_type=jnp.float32)
    before = rows_before(projected)
    extended = jnp.concatenate([before, projected], axis=2)
    run_rows = projected.shape[2]
    convolved = (
        taps[0] * extended[:, :, 2:]
        + taps[1] * extended[:, :, 1:-1]
        + taps[2] * extended[:, :, :-2]
    )
    value_part = convolved[..., :width_d]
    gate_one = convolved[..., width_d : 2 * width_d]
    gate_two = convolved[..., 2 * width_d :]
    spec_one = transform(filter_blocks(filter_one))
    spec_two = transform(filter_blocks(filter_two))
    one_real, one_imag = widen_groups(spec_one, width_d)
    two_real, two_imag = widen_groups(spec_two, width_d)
    value_real, value_imag = transform(value_part)
    y_one = (
        untransform(*complex_mul(one_real, one_imag, value_real, value_imag), False)
        + skip_one * value_part
    )
    gated_mid = gate_one * y_one
    mid_real, mid_imag = transform(gated_mid)
    y_two = (
        untransform(*complex_mul(two_real, two_imag, mid_real, mid_imag), False)
        + skip_two * gated_mid
    )
    product = (gate_two * y_two).astype(jnp.bfloat16)
    output = jnp.einsum("entc,cd->entd", product, w_out, preferred_element_type=jnp.float32).astype(
        jnp.bfloat16
    )
    d_product = jnp.einsum("entd,cd->entc", cot_here, w_out, preferred_element_type=jnp.float32)
    grad_two = d_product * gate_two
    d_gate_two = d_product * y_two
    gtwo_real, gtwo_imag = transform(grad_two)
    d_mid = (
        untransform(*complex_mul(two_real, -two_imag, gtwo_real, gtwo_imag), False)
        + skip_two * grad_two
    )
    filter_two_spec = group_sum(complex_mul(mid_real, -mid_imag, gtwo_real, gtwo_imag), filters)
    filter_two_time = untransform(filter_two_spec[0], filter_two_spec[1], False)[0, 0].T
    grad_one = d_mid * gate_one
    d_gate_one = d_mid * y_one
    gone_real, gone_imag = transform(grad_one)
    d_value = (
        untransform(*complex_mul(one_real, -one_imag, gone_real, gone_imag), False)
        + skip_one * grad_one
    )
    filter_one_spec = group_sum(complex_mul(value_real, -value_imag, gone_real, gone_imag), filters)
    filter_one_time = untransform(filter_one_spec[0], filter_one_spec[1], False)[0, 0].T
    d_convolved = jnp.concatenate([d_value, d_gate_one, d_gate_two], axis=3)
    after = rows_after(d_convolved)
    extended_back = jnp.concatenate([d_convolved, after], axis=2)
    d_projected = (
        taps[0] * extended_back[:, :, :-2]
        + taps[1] * extended_back[:, :, 1:-1]
        + taps[2] * extended_back[:, :, 2:]
    ).astype(jnp.bfloat16)
    d_series = jnp.einsum(
        "entc,dc->entd", d_projected, w_in, preferred_element_type=jnp.float32
    ).astype(jnp.bfloat16)
    local_w_in = jnp.einsum(
        "entd,entc->dc", series_here, d_projected, preferred_element_type=jnp.float32
    )
    local_w_out = jnp.einsum("entc,entd->cd", product, cot_here, preferred_element_type=jnp.float32)
    local_taps = jnp.stack(
        [
            jnp.sum(
                d_convolved * extended[:, :, 2 - offset : 2 - offset + run_rows], axis=(0, 1, 2)
            )
            for offset in range(3)
        ]
    )
    local_skip_one = jnp.sum(grad_one * value_part, axis=(0, 1, 2))
    local_skip_two = jnp.sum(grad_two * gated_mid, axis=(0, 1, 2))
    grad_w_in, grad_w_out, grad_taps, grad_skip_one, grad_skip_two = lax.psum(
        (local_w_in, local_w_out, local_taps, local_skip_one, local_skip_two), ("dp", "seq")
    )
    grad_filter_one, grad_filter_two = (
        lax.psum(filter_one_time.astype(jnp.bfloat16), "dp").astype(jnp.float32),
        lax.psum(filter_two_time.astype(jnp.bfloat16), "dp").astype(jnp.float32),
    )
    output = output.reshape(series_count, block_rows, width_d)
    d_series = d_series.reshape(series_count, block_rows, width_d)
    return (
        output,
        d_series,
        grad_scale * grad_w_in,
        grad_scale * grad_w_out,
        grad_scale * grad_taps,
        grad_scale * grad_skip_one,
        grad_scale * grad_skip_two,
        grad_scale * grad_filter_one,
        grad_scale * grad_filter_two,
    )


def solution(mesh):
    in_specs = (
        P("dp", "seq", None),
        P("dp", "seq", None),
        P(),
        P(),
        P(),
        P(),
        P(),
        P(None, "seq"),
        P(None, "seq"),
    )
    out_specs = (
        P("dp", "seq", None),
        P("dp", "seq", None),
        P(),
        P(),
        P(),
        P(),
        P(),
        P(None, "seq"),
        P(None, "seq"),
    )
    return jax.shard_map(shards, mesh=mesh, in_specs=in_specs, out_specs=out_specs, check_vma=False)
```

profile of v0, /device:TPU:1, one launch (start us, length us, event | category | flops | bytes accessed | tf_op | source)
XLA Modules:
  0.0 1293.6 jit_solution(11738205178397126315)
XLA Ops:
  10.7 9.3 all-to-all-start.4
  89.2 9.1 all-to-all-done.9
  144.8 8.3 all-to-all-done.11
  188.9 8.4 all-to-all-done.14
  231.7 7.3 all-to-all-done.16
  245.4 9.6 all-to-all-done.17
  263.8 7.9 all-to-all-done.18
  283.9 12.2 all_to_all.876
  457.0 7.4 all-to-all-done.34
  516.8 10.7 fusion.14
  540.9 8.3 all-to-all-done.26
  557.4 8.5 all-to-all-done.25
  635.3 7.5 all-to-all-done.38
  651.9 7.5 all-to-all-done.28
  693.9 12.0 all_to_all.877
  835.4 8.3 fusion.12
  874.4 7.4 all-to-all-start.57
  958.3 9.3 all-to-all-done.45
  998.8 8.4 all-to-all-done.47
  1015.1 27.4 %all-reduce.2 = (bf16[8,512]{1,0:T(8,128)(2,1)}, bf16[8,512]{1,0:T(8,128)(2,1)}) all-reduce(bf16[8,512]{1,0:T(8,128)(2,1)S(1)} %bitcast.1449, bf16[8,512]{1,0:T(8,128)(2,1)S(1)} %bitcast.1448), channel_id=1, replica_groups=mesh['dp'=8,'seq'=16] {'dp'}, use_global_device_ids=true, to_apply=%region_12.13 | all-reduce | flops 8192 | bytes 32768 | tf_op jit(solution)/shard_map/psum | solution.py:324
  1046.1 14.8 %all-to-all-start.49 = ((f32[1,16,32,128]{3,2,0,1:T(8,128)}), f32[1,16,32,128]{3,2,0,1:T(8,128)S(1)}, u32[]{:S(2)}, u32[]{:S(2)}) async-start(f32[1,16,32,128]{3,2,0,1:T(8,128)} %copy.829), calls=%async_computation.49 | async-start | bytes 524288 | tf_op jit(solution)/shard_map/all_to_all | solution.py:163
  1062.2 7.4 all-to-all-done.49
  1075.5 66.5 %all-reduce = (f32[3,384]{1,0:T(4,128)S(1)}, f32[128]{0:T(128)S(1)}, f32[128]{0:T(128)S(1)}) all-reduce(f32[3,384]{1,0:T(4,128)S(1)} %pad_maximum_fusion.3, f32[128]{0:T(128)S(1)} %copy-done.70, f32[128]{0:T(128)S(1)} %copy-done.69), channel_id=1, replica_groups=mesh['dp'=8,'seq'=16] {'dp','seq'}, use_global_device_ids=true, to_apply=%region_5.6 | all-reduce | flops 1408 | bytes 11264 | tf_op jit(solution)/shard_map/psum | solution.py:320
  1145.6 137.8 %all-reduce.5.cloned.1.call-done = (f32[128,384]{0,1:T(8,128)}, f32[128,128]{1,0:T(8,128)}) async-done(((f32[128,384]{0,1:T(8,128)}, f32[128,128]{1,0:T(8,128)}), (f32[128,384]{0,1:T(8,128)}, f32[128,128]{1,0:T(8,128)})) %all-reduce.5.cloned.1.call-update) | async-done | bytes 262160 | tf_op jit(solution)/shard_map/psum | solution.py:320
  (628 shorter events, 855.7 us)
Async XLA Ops:
  10.7 17.3 %all-to-all-start.4 = ((f32[16,1,256]{2,1,0:T(1,128)}), f32[16,1,256]{2,1,0:T(1,128)S(1)}, u32[]{:S(2)}, u32[]{:S(2)}) async-start(f32[16,1,256]{2,1,0:T(1,128)} %reshape.1187), calls=%async_computation.4 | async-start | bytes 32768 | tf_op jit(solution)/shard_map/all_to_all | solution.py:150
  21.2 27.8 %collective-permute-start = (f32[1,1,2,384]{3,2,1,0:T(2,128)S(1)}, f32[1,1,2,384]{3,2,1,0:T(2,128)S(1)}, u32[]{:S(2)}, u32[]{:S(2)}) collective-permute-start(f32[1,1,2,384]{3,2,1,0:T(2,128)S(1)} %slice.53), channel_id=1, source_target_pairs={{0,1},{1,2},{2,3},{3,4},{4,5},{5,6},{6,7},{7,8},{8,9},{9,10},{10,1... | collective-permute-start | bytes 9224 | tf_op jit(solution)/shard_map/ppermute | solution.py:13
  222.0 17.0 %all-to-all-start.16 = ((f32[1,2,512,128]{3,1,0,2:T(2,128)}), f32[1,2,512,128]{3,1,0,2:T(2,128)}, u32[]{:S(2)}, u32[]{:S(2)}) async-start(f32[1,2,512,128]{3,1,0,2:T(2,128)} %copy.682), calls=%async_computation.16 | async-start | bytes 1048576 | tf_op jit(solution)/shard_map/all_to_all | solution.py:159
  296.1 19.9 %all-to-all-start.30 = ((f32[1,1,512,128]{3,1,0,2:T(1,128)}), f32[1,1,512,128]{3,1,0,2:T(1,128)}, u32[]{:S(2)}, u32[]{:S(2)}) async-start(f32[1,1,512,128]{3,1,0,2:T(1,128)} %bitcast.259), calls=%async_computation.30 | async-start | bytes 524288 | tf_op jit(solution)/shard_map/all_to_all | solution.py:150
  330.7 17.8 %all-to-all-start.31 = ((f32[1,32,32,128]{3,2,0,1:T(8,128)}), f32[1,32,32,128]{3,2,0,1:T(8,128)}, u32[]{:S(2)}, u32[]{:S(2)}) async-start(f32[1,32,32,128]{3,2,0,1:T(8,128)} %copy.745), calls=%async_computation.31 | async-start | bytes 1048576 | tf_op jit(solution)/shard_map/all_to_all | solution.py:142
  348.5 19.5 %all-to-all-start.32 = ((f32[1,32,32,128]{3,2,0,1:T(8,128)}), f32[1,32,32,128]{3,2,0,1:T(8,128)}, u32[]{:S(2)}, u32[]{:S(2)}) async-start(f32[1,32,32,128]{3,2,0,1:T(8,128)} %copy.748), calls=%async_computation.32 | async-start | bytes 1048576 | tf_op jit(solution)/shard_map/all_to_all | solution.py:143
  368.1 18.7 %all-to-all-start.21 = ((f32[1,32,32,128]{3,2,0,1:T(8,128)}), f32[1,32,32,128]{3,2,0,1:T(8,128)}, u32[]{:S(2)}, u32[]{:S(2)}) async-start(f32[1,32,32,128]{3,2,0,1:T(8,128)} %copy.700), calls=%async_computation.21 | async-start | bytes 1048576 | tf_op jit(solution)/shard_map/all_to_all | solution.py:143
  386.8 16.6 %all-to-all-start.20 = ((f32[1,32,32,128]{3,2,0,1:T(8,128)}), f32[1,32,32,128]{3,2,0,1:T(8,128)}, u32[]{:S(2)}, u32[]{:S(2)}) async-start(f32[1,32,32,128]{3,2,0,1:T(8,128)} %copy.697), calls=%async_computation.20 | async-start | bytes 1048576 | tf_op jit(solution)/shard_map/all_to_all | solution.py:142
  447.7 16.6 %all-to-all-start.34 = ((f32[1,2,512,128]{3,1,0,2:T(2,128)}), f32[1,2,512,128]{3,1,0,2:T(2,128)}, u32[]{:S(2)}, u32[]{:S(2)}) async-start(f32[1,2,512,128]{3,1,0,2:T(2,128)} %copy.763), calls=%async_computation.34 | async-start | bytes 1048576 | tf_op jit(solution)/shard_map/all_to_all | solution.py:173
  464.3 17.0 %all-to-all-start.24 = ((f32[1,2,512,128]{3,1,0,2:T(2,128)}), f32[1,2,512,128]{3,1,0,2:T(2,128)}, u32[]{:S(2)}, u32[]{:S(2)}) async-start(f32[1,2,512,128]{3,1,0,2:T(2,128)} %copy.719), calls=%async_computation.24 | async-start | bytes 1048576 | tf_op jit(solution)/shard_map/all_to_all | solution.py:173
  481.4 22.5 %all-to-all-start.22 = ((f32[1,2,512,128]{3,1,0,2:T(2,128)}), f32[1,2,512,128]{3,1,0,2:T(2,128)}, u32[]{:S(2)}, u32[]{:S(2)}) async-start(f32[1,2,512,128]{3,1,0,2:T(2,128)} %copy.708), calls=%async_computation.22 | async-start | bytes 1048576 | tf_op jit(solution)/shard_map/all_to_all | solution.py:172
  530.6 18.7 %all-to-all-start.26 = ((f32[1,32,32,128]{3,2,0,1:T(8,128)}), f32[1,32,32,128]{3,2,0,1:T(8,128)S(1)}, u32[]{:S(2)}, u32[]{:S(2)}) async-start(f32[1,32,32,128]{3,2,0,1:T(8,128)} %copy.725), calls=%async_computation.26 | async-start | bytes 1048576 | tf_op jit(solution)/shard_map/all_to_all | solution.py:183
  549.3 16.6 %all-to-all-start.25 = ((f32[1,32,32,128]{3,2,0,1:T(8,128)}), f32[1,32,32,128]{3,2,0,1:T(8,128)}, u32[]{:S(2)}, u32[]{:S(2)}) async-start(f32[1,32,32,128]{3,2,0,1:T(8,128)} %copy.723), calls=%async_computation.25 | async-start | bytes 1048576 | tf_op jit(solution)/shard_map/all_to_all | solution.py:182
  565.9 16.8 %all-to-all-start.36 = ((f32[1,32,32,128]{3,2,0,1:T(8,128)}), f32[1,32,32,128]{3,2,0,1:T(8,128)}, u32[]{:S(2)}, u32[]{:S(2)}) async-start(f32[1,32,32,128]{3,2,0,1:T(8,128)} %copy.769), calls=%async_computation.36 | async-start | bytes 1048576 | tf_op jit(solution)/shard_map/all_to_all | solution.py:183
  609.3 16.8 %all-to-all-start.37 = ((f32[1,2,512,128]{3,1,0,2:T(2,128)}), f32[1,2,512,128]{3,1,0,2:T(2,128)}, u32[]{:S(2)}, u32[]{:S(2)}) async-start(f32[1,2,512,128]{3,1,0,2:T(2,128)} %copy.774), calls=%async_computation.37 | async-start | bytes 1048576 | tf_op jit(solution)/shard_map/all_to_all | solution.py:159
  626.1 16.6 %all-to-all-start.38 = ((f32[1,2,512,128]{3,1,0,2:T(2,128)}), f32[1,2,512,128]{3,1,0,2:T(2,128)}, u32[]{:S(2)}, u32[]{:S(2)}) async-start(f32[1,2,512,128]{3,1,0,2:T(2,128)} %copy.780), calls=%async_computation.38 | async-start | bytes 1048576 | tf_op jit(solution)/shard_map/all_to_all | solution.py:160
  642.7 16.6 %all-to-all-start.28 = ((f32[1,2,512,128]{3,1,0,2:T(2,128)}), f32[1,2,512,128]{3,1,0,2:T(2,128)}, u32[]{:S(2)}, u32[]{:S(2)}) async-start(f32[1,2,512,128]{3,1,0,2:T(2,128)} %copy.736), calls=%async_computation.28 | async-start | bytes 1048576 | tf_op jit(solution)/shard_map/all_to_all | solution.py:160
  708.8 17.2 %all-to-all-start.40 = ((f32[1,1,512,128]{3,1,0,2:T(1,128)}), f32[1,1,512,128]{3,1,0,2:T(1,128)}, u32[]{:S(2)}, u32[]{:S(2)}) async-start(f32[1,1,512,128]{3,1,0,2:T(1,128)} %bitcast.1339), calls=%async_computation.40 | async-start | bytes 524288 | tf_op jit(solution)/shard_map/all_to_all | solution.py:150
  792.6 18.3 %all-to-all-start.43 = ((f32[1,2,512,128]{3,1,0,2:T(2,128)}), f32[1,2,512,128]{3,1,0,2:T(2,128)}, u32[]{:S(2)}, u32[]{:S(2)}) async-start(f32[1,2,512,128]{3,1,0,2:T(2,128)} %copy.800), calls=%async_computation.43 | async-start | bytes 1048576 | tf_op jit(solution)/shard_map/all_to_all | solution.py:172
  911.1 21.9 %all-to-all-start.52 = ((f32[16,1,512]{2,1,0:T(1,128)}), f32[16,1,512]{2,1,0:T(1,128)}, u32[]{:S(2)}, u32[]{:S(2)}) async-start(f32[16,1,512]{2,1,0:T(1,128)} %reshape.1213), calls=%async_computation.52 | async-start | bytes 65536 | tf_op jit(solution)/shard_map/all_to_all | solution.py:159
  933.1 18.7 %all-to-all-start.46 = ((f32[1,32,32,128]{3,2,0,1:T(8,128)}), f32[1,32,32,128]{3,2,0,1:T(8,128)S(1)}, u32[]{:S(2)}, u32[]{:S(2)}) async-start(f32[1,32,32,128]{3,2,0,1:T(8,128)} %copy.813), calls=%async_computation.46 | async-start | bytes 1048576 | tf_op jit(solution)/shard_map/all_to_all | solution.py:183
  1007.2 35.4 %all-to-all-start.48 = ((f32[1,2,512,128]{3,1,0,2:T(2,128)}), f32[1,2,512,128]{3,1,0,2:T(2,128)S(1)}, u32[]{:S(2)}, u32[]{:S(2)}) async-start(f32[1,2,512,128]{3,1,0,2:T(2,128)} %copy.824), calls=%async_computation.48 | async-start | bytes 1048576 | tf_op jit(solution)/shard_map/all_to_all | solution.py:160
  1046.1 23.5 %all-to-all-start.49 = ((f32[1,16,32,128]{3,2,0,1:T(8,128)}), f32[1,16,32,128]{3,2,0,1:T(8,128)S(1)}, u32[]{:S(2)}, u32[]{:S(2)}) async-start(f32[1,16,32,128]{3,2,0,1:T(8,128)} %copy.829), calls=%async_computation.49 | async-start | bytes 524288 | tf_op jit(solution)/shard_map/all_to_all | solution.py:163
  1060.9 222.4 %all-reduce.5.cloned.1.call-start = ((), (), s32[]{:S(2)}) async-start(), calls=%async_computation.60 | async-start | bytes 524288 | tf_op jit(solution)/shard_map/psum | solution.py:320
  (108 other events, 1326.8 us)
Sparse Core Ops, SparseCore 0:
  1144.8 138.5 all-reduce.4
where the time goes:
time: 1310 us; the launch traced here: 1290 us
  waiting for transfers between devices  427 us (33%)
  starting transfers between devices  315 us (24%)
  local copies, waits for them, and re-layouts  193 us (15%)
  matrix products  149 us (11%)
  blocking collectives  118 us (9%)
  other arithmetic  75 us (6%)
  between operations  16.5 us (1%)
    psum x1, waiting for transfers between devices, shards(): lax.psum((local_w_in, local_w_out, local_taps, local_skip_one, local_skip...  138 us
    psum x1, blocking collectives, shards(): lax.psum((local_w_in, local_w_out, local_taps, local_skip_one, local_skip...  66.5 us
    unnamed x186, local copies, waits for them, and re-layouts  50.7 us
    all_to_all x6, waiting for transfers between devices, restore_spectrum(): lax.all_to_all(real_part, 'seq', split_axis=1, concat_axis=2, tiled=True)  38.3 us
    all_to_all x6, starting transfers between devices, restore_spectrum(): lax.all_to_all(imag_part, 'seq', split_axis=1, concat_axis=2, tiled=True)  37.1 us
    all_to_all x6, waiting for transfers between devices, signal(): lax.all_to_all(imag_part, 'seq', split_axis=2, concat_axis=1, tiled=True)  34.4 us
    all_to_all x5, starting transfers between devices, signal(): lax.all_to_all(columns, 'seq', split_axis=1, concat_axis=2, tiled=True)  34.3 us
    all_to_all x6, waiting for transfers between devices, order_spectrum(): lax.all_to_all(imag_part, 'seq', split_axis=2, concat_axis=1, tiled=True)  33.6 us
  transfers between devices with their start and end apart: 61, of which 52 were waited for; matrix products, arithmetic and copies ran while one was open for 23% of the time, Pallas kernels for 0%

commit v1 on v0

--- a/solution.py
+++ b/solution.py
@@ -321,7 +321,9 @@
         (local_w_in, local_w_out, local_taps, local_skip_one, local_skip_two), ("dp", "seq")
     )
     grad_filter_one, grad_filter_two = (
-        lax.psum(filter_one_time.astype(jnp.bfloat16), "dp").astype(jnp.float32),
+        jnp.sum(lax.all_gather(filter_one_time.astype(jnp.bfloat16), "dp"), axis=0).astype(
+            jnp.float32
+        ),
         lax.psum(filter_two_time.astype(jnp.bfloat16), "dp").astype(jnp.float32),
     )
     output = output.reshape(series_count, block_rows, width_d)

time: 1310 us -> 1330 us (1.015)
    all_gather x0 -> x1, blocking collectives: none -> 24.1 us  [shards(): lax.all_gather(filter_one_time.astype(jnp.bfloat16), 'dp')]
    unnamed x186 -> x182, local copies, waits for them, and re-layouts: 50.7 us -> 50.7 us
where the time goes in v1:
time: 1330 us; the launch traced here: 1310 us
  waiting for transfers between devices  426 us (32%)
  starting transfers between devices  318 us (24%)
  local copies, waits for them, and re-layouts  193 us (15%)
  matrix products  150 us (11%)
  blocking collectives  131 us (10%)
  other arithmetic  75 us (6%)
  between operations  16.5 us (1%)
    psum x1, waiting for transfers between devices, shards(): lax.psum((local_w_in, local_w_out, local_taps, local_skip_one, local_skip...  138 us
    psum x1, blocking collectives, shards(): lax.psum((local_w_in, local_w_out, local_taps, local_skip_one, local_skip...  66.5 us
    unnamed x182, local copies, waits for them, and re-layouts  50.7 us
    all_to_all x6, waiting for transfers between devices, restore_spectrum(): lax.all_to_all(real_part, 'seq', split_axis=1, concat_axis=2, tiled=True)  38.3 us
    all_to_all x6, starting transfers between devices, restore_spectrum(): lax.all_to_all(imag_part, 'seq', split_axis=1, concat_axis=2, tiled=True)  37.1 us
    all_to_all x5, starting transfers between devices, signal(): lax.all_to_all(columns, 'seq', split_axis=1, concat_axis=2, tiled=True)  37 us
    all_to_all x6, waiting for transfers between devices, signal(): lax.all_to_all(imag_part, 'seq', split_axis=2, concat_axis=1, tiled=True)  34.4 us
    all_to_all x6, waiting for transfers between devices, order_spectrum(): lax.all_to_all(imag_part, 'seq', split_axis=2, concat_axis=1, tiled=True)  33.5 us
  transfers between devices with their start and end apart: 61, of which 52 were waited for; matrix products, arithmetic and copies ran while one was open for 23% of the time, Pallas kernels for 0%

profile of v1, /device:TPU:1, one launch (start us, length us, event | category | flops | bytes accessed | tf_op | source)
XLA Modules:
  0.0 1308.6 jit_solution(15444972497676877259)
XLA Ops:
  10.7 9.3 all-to-all-start.4
  89.1 9.2 all-to-all-done.9
  144.8 8.3 all-to-all-done.11
  188.9 8.4 all-to-all-done.14
  231.7 7.4 all-to-all-done.16
  245.4 9.6 all-to-all-done.17
  263.8 7.9 all-to-all-done.18
  283.9 12.2 all_to_all.876
  457.0 7.3 all-to-all-done.34
  516.8 10.7 fusion.14
  540.9 8.3 all-to-all-done.26
  557.4 8.5 all-to-all-done.25
  635.3 7.5 all-to-all-done.38
  651.9 7.5 all-to-all-done.28
  693.9 12.0 all_to_all.877
  835.4 8.3 fusion.12
  874.4 7.4 all-to-all-start.57
  958.4 9.3 all-to-all-done.45
  1014.2 15.9 %psum.47 = bf16[8,512]{1,0:T(8,128)(2,1)S(1)} all-reduce(bf16[8,512]{1,0:T(8,128)(2,1)S(1)} %bitcast.1451), channel_id=1, replica_groups=mesh['dp'=8,'seq'=16] {'dp'}, use_global_device_ids=true, to_apply=%region_15.16 | all-reduce | flops 4096 | bytes 16384 | tf_op jit(solution)/shard_map/psum | solution.py:327
  1030.1 24.1 %all-gather = bf16[64,512]{1,0:T(8,128)(2,1)} all-gather(bf16[8,512]{1,0:T(8,128)(2,1)S(1)} %bitcast.1450), channel_id=2, replica_groups=mesh['dp'=8,'seq'=16] {'dp'}, dimensions={0}, use_global_device_ids=true | all-gather | bytes 73728 | tf_op jit(solution)/shard_map/all_gather | solution.py:324
  1058.4 17.5 %all-to-all-start.49 = ((f32[1,16,32,128]{3,2,0,1:T(8,128)}), f32[1,16,32,128]{3,2,0,1:T(8,128)S(1)}, u32[]{:S(2)}, u32[]{:S(2)}) async-start(f32[1,16,32,128]{3,2,0,1:T(8,128)} %copy.829), calls=%async_computation.49 | async-start | bytes 524288 | tf_op jit(solution)/shard_map/all_to_all | solution.py:163
  1076.6 8.0 all-to-all-done.49
  1090.4 66.5 %all-reduce = (f32[3,384]{1,0:T(4,128)S(1)}, f32[128]{0:T(128)S(1)}, f32[128]{0:T(128)S(1)}) all-reduce(f32[3,384]{1,0:T(4,128)S(1)} %pad_maximum_fusion.3, f32[128]{0:T(128)S(1)} %copy-done.68, f32[128]{0:T(128)S(1)} %copy-done.67), channel_id=1, replica_groups=mesh['dp'=8,'seq'=16] {'dp','seq'}, use_global_device_ids=true, to_apply=%region_5.6 | all-reduce | flops 1408 | bytes 11264 | tf_op jit(solution)/shard_map/psum | solution.py:320
  1160.6 137.8 %all-reduce.4.cloned.1.call-done = (f32[128,384]{0,1:T(8,128)}, f32[128,128]{1,0:T(8,128)}) async-done(((f32[128,384]{0,1:T(8,128)}, f32[128,128]{1,0:T(8,128)}), (f32[128,384]{0,1:T(8,128)}, f32[128,128]{1,0:T(8,128)})) %all-reduce.4.cloned.1.call-update) | async-done | bytes 262160 | tf_op jit(solution)/shard_map/psum | solution.py:320
  (626 shorter events, 863.2 us)
Async XLA Ops:
  10.7 17.3 %all-to-all-start.4 = ((f32[16,1,256]{2,1,0:T(1,128)}), f32[16,1,256]{2,1,0:T(1,128)S(1)}, u32[]{:S(2)}, u32[]{:S(2)}) async-start(f32[16,1,256]{2,1,0:T(1,128)} %reshape.1188), calls=%async_computation.4 | async-start | bytes 32768 | tf_op jit(solution)/shard_map/all_to_all | solution.py:150
  21.2 27.8 %collective-permute-start = (f32[1,1,2,384]{3,2,1,0:T(2,128)S(1)}, f32[1,1,2,384]{3,2,1,0:T(2,128)S(1)}, u32[]{:S(2)}, u32[]{:S(2)}) collective-permute-start(f32[1,1,2,384]{3,2,1,0:T(2,128)S(1)} %slice.53), channel_id=1, source_target_pairs={{0,1},{1,2},{2,3},{3,4},{4,5},{5,6},{6,7},{7,8},{8,9},{9,10},{10,1... | collective-permute-start | bytes 9224 | tf_op jit(solution)/shard_map/ppermute | solution.py:13
  197.3 16.6 %all-to-all-start.15 = ((f32[1,32,32,128]{3,2,0,1:T(8,128)}), f32[1,32,32,128]{3,2,0,1:T(8,128)}, u32[]{:S(2)}, u32[]{:S(2)}) async-start(f32[1,32,32,128]{3,2,0,1:T(8,128)} %copy.675), calls=%async_computation.15 | async-start | bytes 1048576 | tf_op jit(solution)/shard_map/all_to_all | solution.py:183
  222.1 17.0 %all-to-all-start.16 = ((f32[1,2,512,128]{3,1,0,2:T(2,128)}), f32[1,2,512,128]{3,1,0,2:T(2,128)}, u32[]{:S(2)}, u32[]{:S(2)}) async-start(f32[1,2,512,128]{3,1,0,2:T(2,128)} %copy.682), calls=%async_computation.16 | async-start | bytes 1048576 | tf_op jit(solution)/shard_map/all_to_all | solution.py:159
  296.2 19.9 %all-to-all-start.30 = ((f32[1,1,512,128]{3,1,0,2:T(1,128)}), f32[1,1,512,128]{3,1,0,2:T(1,128)}, u32[]{:S(2)}, u32[]{:S(2)}) async-start(f32[1,1,512,128]{3,1,0,2:T(1,128)} %bitcast.259), calls=%async_computation.30 | async-start | bytes 524288 | tf_op jit(solution)/shard_map/all_to_all | solution.py:150
  330.8 17.8 %all-to-all-start.31 = ((f32[1,32,32,128]{3,2,0,1:T(8,128)}), f32[1,32,32,128]{3,2,0,1:T(8,128)}, u32[]{:S(2)}, u32[]{:S(2)}) async-start(f32[1,32,32,128]{3,2,0,1:T(8,128)} %copy.745), calls=%async_computation.31 | async-start | bytes 1048576 | tf_op jit(solution)/shard_map/all_to_all | solution.py:142
  348.6 19.5 %all-to-all-start.32 = ((f32[1,32,32,128]{3,2,0,1:T(8,128)}), f32[1,32,32,128]{3,2,0,1:T(8,128)}, u32[]{:S(2)}, u32[]{:S(2)}) async-start(f32[1,32,32,128]{3,2,0,1:T(8,128)} %copy.748), calls=%async_computation.32 | async-start | bytes 1048576 | tf_op jit(solution)/shard_map/all_to_all | solution.py:143
  368.1 18.7 %all-to-all-start.21 = ((f32[1,32,32,128]{3,2,0,1:T(8,128)}), f32[1,32,32,128]{3,2,0,1:T(8,128)}, u32[]{:S(2)}, u32[]{:S(2)}) async-start(f32[1,32,32,128]{3,2,0,1:T(8,128)} %copy.700), calls=%async_computation.21 | async-start | bytes 1048576 | tf_op jit(solution)/shard_map/all_to_all | solution.py:143
  386.8 16.6 %all-to-all-start.20 = ((f32[1,32,32,128]{3,2,0,1:T(8,128)}), f32[1,32,32,128]{3,2,0,1:T(8,128)}, u32[]{:S(2)}, u32[]{:S(2)}) async-start(f32[1,32,32,128]{3,2,0,1:T(8,128)} %copy.697), calls=%async_computation.20 | async-start | bytes 1048576 | tf_op jit(solution)/shard_map/all_to_all | solution.py:142
  464.3 17.0 %all-to-all-start.24 = ((f32[1,2,512,128]{3,1,0,2:T(2,128)}), f32[1,2,512,128]{3,1,0,2:T(2,128)}, u32[]{:S(2)}, u32[]{:S(2)}) async-start(f32[1,2,512,128]{3,1,0,2:T(2,128)} %copy.719), calls=%async_computation.24 | async-start | bytes 1048576 | tf_op jit(solution)/shard_map/all_to_all | solution.py:173
  481.4 22.5 %all-to-all-start.22 = ((f32[1,2,512,128]{3,1,0,2:T(2,128)}), f32[1,2,512,128]{3,1,0,2:T(2,128)}, u32[]{:S(2)}, u32[]{:S(2)}) async-start(f32[1,2,512,128]{3,1,0,2:T(2,128)} %copy.708), calls=%async_computation.22 | async-start | bytes 1048576 | tf_op jit(solution)/shard_map/all_to_all | solution.py:172
  530.6 18.7 %all-to-all-start.26 = ((f32[1,32,32,128]{3,2,0,1:T(8,128)}), f32[1,32,32,128]{3,2,0,1:T(8,128)S(1)}, u32[]{:S(2)}, u32[]{:S(2)}) async-start(f32[1,32,32,128]{3,2,0,1:T(8,128)} %copy.725), calls=%async_computation.26 | async-start | bytes 1048576 | tf_op jit(solution)/shard_map/all_to_all | solution.py:183
  549.2 16.6 %all-to-all-start.25 = ((f32[1,32,32,128]{3,2,0,1:T(8,128)}), f32[1,32,32,128]{3,2,0,1:T(8,128)}, u32[]{:S(2)}, u32[]{:S(2)}) async-start(f32[1,32,32,128]{3,2,0,1:T(8,128)} %copy.723), calls=%async_computation.25 | async-start | bytes 1048576 | tf_op jit(solution)/shard_map/all_to_all | solution.py:182
  565.9 16.8 %all-to-all-start.36 = ((f32[1,32,32,128]{3,2,0,1:T(8,128)}), f32[1,32,32,128]{3,2,0,1:T(8,128)}, u32[]{:S(2)}, u32[]{:S(2)}) async-start(f32[1,32,32,128]{3,2,0,1:T(8,128)} %copy.769), calls=%async_computation.36 | async-start | bytes 1048576 | tf_op jit(solution)/shard_map/all_to_all | solution.py:183
  609.3 16.8 %all-to-all-start.37 = ((f32[1,2,512,128]{3,1,0,2:T(2,128)}), f32[1,2,512,128]{3,1,0,2:T(2,128)}, u32[]{:S(2)}, u32[]{:S(2)}) async-start(f32[1,2,512,128]{3,1,0,2:T(2,128)} %copy.774), calls=%async_computation.37 | async-start | bytes 1048576 | tf_op jit(solution)/shard_map/all_to_all | solution.py:159
  626.1 16.6 %all-to-all-start.38 = ((f32[1,2,512,128]{3,1,0,2:T(2,128)}), f32[1,2,512,128]{3,1,0,2:T(2,128)}, u32[]{:S(2)}, u32[]{:S(2)}) async-start(f32[1,2,512,128]{3,1,0,2:T(2,128)} %copy.780), calls=%async_computation.38 | async-start | bytes 1048576 | tf_op jit(solution)/shard_map/all_to_all | solution.py:160
  708.8 17.1 %all-to-all-start.40 = ((f32[1,1,512,128]{3,1,0,2:T(1,128)}), f32[1,1,512,128]{3,1,0,2:T(1,128)}, u32[]{:S(2)}, u32[]{:S(2)}) async-start(f32[1,1,512,128]{3,1,0,2:T(1,128)} %bitcast.1341), calls=%async_computation.40 | async-start | bytes 524288 | tf_op jit(solution)/shard_map/all_to_all | solution.py:150
  768.4 16.6 %all-to-all-start.42 = ((f32[1,32,32,128]{3,2,0,1:T(8,128)}), f32[1,32,32,128]{3,2,0,1:T(8,128)}, u32[]{:S(2)}, u32[]{:S(2)}) async-start(f32[1,32,32,128]{3,2,0,1:T(8,128)} %copy.792), calls=%async_computation.42 | async-start | bytes 1048576 | tf_op jit(solution)/shard_map/all_to_all | solution.py:143
  792.7 18.3 %all-to-all-start.43 = ((f32[1,2,512,128]{3,1,0,2:T(2,128)}), f32[1,2,512,128]{3,1,0,2:T(2,128)}, u32[]{:S(2)}, u32[]{:S(2)}) async-start(f32[1,2,512,128]{3,1,0,2:T(2,128)} %copy.800), calls=%async_computation.43 | async-start | bytes 1048576 | tf_op jit(solution)/shard_map/all_to_all | solution.py:172
  911.1 22.0 %all-to-all-start.52 = ((f32[16,1,512]{2,1,0:T(1,128)}), f32[16,1,512]{2,1,0:T(1,128)}, u32[]{:S(2)}, u32[]{:S(2)}) async-start(f32[16,1,512]{2,1,0:T(1,128)} %reshape.1214), calls=%async_computation.52 | async-start | bytes 65536 | tf_op jit(solution)/shard_map/all_to_all | solution.py:159
  933.1 18.7 %all-to-all-start.46 = ((f32[1,32,32,128]{3,2,0,1:T(8,128)}), f32[1,32,32,128]{3,2,0,1:T(8,128)S(1)}, u32[]{:S(2)}, u32[]{:S(2)}) async-start(f32[1,32,32,128]{3,2,0,1:T(8,128)} %copy.813), calls=%async_computation.46 | async-start | bytes 1048576 | tf_op jit(solution)/shard_map/all_to_all | solution.py:183
  1007.2 47.8 %all-to-all-start.48 = ((f32[1,2,512,128]{3,1,0,2:T(2,128)}), f32[1,2,512,128]{3,1,0,2:T(2,128)S(1)}, u32[]{:S(2)}, u32[]{:S(2)}) async-start(f32[1,2,512,128]{3,1,0,2:T(2,128)} %copy.824), calls=%async_computation.48 | async-start | bytes 1048576 | tf_op jit(solution)/shard_map/all_to_all | solution.py:160
  1058.4 26.1 %all-to-all-start.49 = ((f32[1,16,32,128]{3,2,0,1:T(8,128)}), f32[1,16,32,128]{3,2,0,1:T(8,128)S(1)}, u32[]{:S(2)}, u32[]{:S(2)}) async-start(f32[1,16,32,128]{3,2,0,1:T(8,128)} %copy.829), calls=%async_computation.49 | async-start | bytes 524288 | tf_op jit(solution)/shard_map/all_to_all | solution.py:163
  1075.9 222.5 %all-reduce.4.cloned.1.call-start = ((), (), s32[]{:S(2)}) async-start(), calls=%async_computation.60 | async-start | bytes 524288 | tf_op jit(solution)/shard_map/psum | solution.py:320
  (106 other events, 1298.2 us)
Sparse Core Ops, SparseCore 0:
  1159.8 138.5 all-reduce.3
